TPU v7x, 128 devices: a whole 4x4x4 slice. The times are simulated.
128 devices in a mesh: wide: 16 (over y_lo, x, core), narrow: 8 (over z, y_hi).
Axes of the slice: x: 4, y: 4 (y_hi: 2, y_lo: 2; y = y_hi * 2 + y_lo), z: 4, core: 2. Of those that a mesh axis runs over, the one named last changes fastest.
Arguments:
- heads_output: bfloat16 [1024, 8192], P('narrow', 'wide'), may hold values from -6 to 6
- residual_in: bfloat16 [1024, 16384], P('wide', 'narrow'), may hold values from -6 to 6
- out_weight: bfloat16 [8192, 16384], P('wide', 'narrow'), may hold values from -0.0625 to 0.0625
- norm_gain: float32 [16384], P('narrow'), may hold values from 0.1 to 1.9
- gate_weight: bfloat16 [16384, 26624], P('narrow', 'wide'), may hold values from -0.046875 to 0.046875
- up_weight: bfloat16 [16384, 26624], P('narrow', 'wide'), may hold values from -0.046875 to 0.046875
Outputs:
- residual: float32 [1024, 16384], P('wide', 'narrow')
- hidden: float32 [1024, 26624], P('narrow', 'wide')
All inputs are finite; a program needn't handle non-finite values.
Results may differ from a plain program's by a relative error of at most 0.0041.
Values may be sent and summed in bfloat16 or wider, within the bound.
A program may use at most 128 MiB of HBM per device.

v0:
```python
import jax
import jax.numpy as jnp
from jax import lax
from jax.sharding import PartitionSpec as P

D = 16384


def norm_scale(squares):
    return 1.0 / jnp.sqrt(squares / D + 1e-05)


def on_device(heads_output, residual_in, out_weight, norm_gain, gate_weight, up_weight):
    gathered = lax.all_gather(heads_output, "narrow", axis=0, tiled=True)
    row_count = residual_in.shape[0]
    offset = lax.axis_index("wide") * row_count
    terms = jnp.dot(gathered, out_weight, preferred_element_type=jnp.float32)
    placed = lax.dynamic_update_slice_in_dim(
        jnp.zeros_like(terms), residual_in.astype(jnp.float32), offset, 0
    )
    total = lax.psum(terms + placed, "wide")
    squares = lax.psum(jnp.sum(total * total, axis=1), "narrow")
    normed = (total * norm_scale(squares)[:, None] * norm_gain).astype(jnp.bfloat16)
    residual = lax.dynamic_slice_in_dim(total, offset, row_count, 0)
    gate_part = jnp.dot(normed, gate_weight, preferred_element_type=jnp.float32)
    up_part = jnp.dot(normed, up_weight, preferred_element_type=jnp.float32)
    gate, up_sum = (
        lax.psum_scatter(gate_part, "narrow", scatter_dimension=0, tiled=True),
        lax.psum_scatter(up_part, "narrow", scatter_dimension=0, tiled=True),
    )
    hidden = jax.nn.silu(gate) * up_sum
    return (residual, hidden)


def solution(mesh):
    in_specs = (
        P("narrow", "wide"),
        P("wide", "narrow"),
        P("wide", "narrow"),
        P("narrow"),
        P("narrow", "wide"),
        P("narrow", "wide"),
    )
    out_specs = (P("wide", "narrow"), P("narrow", "wide"))
    return jax.shard_map(
        on_device, mesh=mesh, in_specs=in_specs, out_specs=out_specs, check_vma=False
    )
```

profile of v0, /device:TPU:1, one launch (start us, length us, event | category | flops | bytes accessed | tf_op | source)
XLA Modules:
  0.0 463.2 jit_solution(4616436277414190073)
XLA Ops:
  7.2 0.0 copy-start
  7.2 0.0 copy-start.1
  7.2 0.0 all-gather.2.cloned.1.call-start
  7.2 0.7 all-gather.2.cloned.1.call-update
  7.9 0.0 all-reduce.2.cloned.1.call-start
  8.0 50.9 %all-gather.2.cloned.1.call-done = bf16[1024,512]{1,0:T(8,128)(2,1)} async-done(((bf16[128,512]{1,0:T(8,128)(2,1)}), bf16[1024,512]{1,0:T(8,128)(2,1)}) %all-gather.2.cloned.1.call-update) | async-done | bytes 1048592 | tf_op jit(solution)/shard_map/all_gather | solution.py:14
  58.8 0.0 copy-done
  58.8 6.8 %fusion.2 = f32[1024,2048]{1,0:T(8,128)} fusion(bf16[1024,512]{1,0:T(8,128)(2,1)} %all-gather.2.cloned.1.call-done, bf16[512,2048]{1,0:T(8,128)(2,1)S(1)} %copy-done), kind=kOutput, calls=%fused_computation.8 | convolution fusion | flops 2147483648 | bytes 11534336 | tf_op jit(solution)/shard_map/dot_general | solution.py:17
  65.6 0.0 copy-done.1
  65.6 2.0 add_dynamic-update-slice_fusion
  67.6 0.0 copy-start.2
  67.6 0.0 all-reduce.2.cloned.1.call-update
  67.6 0.0 reduce-scatter.5.cloned.1.call-start
  67.7 141.2 %all-reduce.2.cloned.1.call-done = f32[1024,2048]{1,0:T(8,128)} async-done(((f32[1024,2048]{1,0:T(8,128)}), f32[1024,2048]{1,0:T(8,128)}) %all-reduce.2.cloned.1.call-update) | async-done | bytes 8388624 | tf_op jit(solution)/shard_map/psum | solution.py:21
  208.8 4.0 multiply_reduce_fusion
  212.8 20.4 %psum.15 = f32[1024]{0:T(1024)S(1)} all-reduce(f32[1024]{0:T(1024)S(1)} %multiply_reduce_fusion), channel_id=1, replica_groups=mesh['wide'=16,'narrow'=8] {'narrow'}, use_global_device_ids=true, to_apply=%region_2.0 | all-reduce | flops 1024 | bytes 8192 | tf_op jit(solution)/shard_map/psum | solution.py:22
  233.2 0.0 copy-done.2
  233.2 14.2 %fusion = f32[1024,1664]{1,0:T(8,128)} fusion(bf16[2048,1664]{1,0:T(8,128)(2,1)} %param.11, f32[1024,2048]{1,0:T(8,128)} %all-reduce.2.cloned.1.call-done, f32[2048]{0:T(1024)S(1)} %copy-done.2, f32[1024]{0:T(1024)S(1)} %add_rsqrt_fusion), kind=kOutput, calls=%fused_computation.6 | convolution fusion | flops 6985613312 | bytes 22032384 | tf_op jit(solution)/shard_map/dot_general | solution.py:26
  247.5 0.0 reduce-scatter.5.cloned.1.call-update
  247.5 0.0 reduce-scatter.3.cloned.1.call-start
  247.5 14.2 %fusion.1 = f32[1024,1664]{1,0:T(8,128)} fusion(bf16[2048,1664]{1,0:T(8,128)(2,1)} %param.10, f32[1024,2048]{1,0:T(8,128)} %all-reduce.2.cloned.1.call-done, f32[2048]{0:T(1024)S(1)} %copy-done.2, f32[1024]{0:T(1024)S(1)} %add_rsqrt_fusion), kind=kOutput, calls=%fused_computation.7 | convolution fusion | flops 6985613312 | bytes 22032384 | tf_op jit(solution)/shard_map/dot_general | solution.py:25
  261.7 0.0 reduce-scatter.3.cloned.1.call-update
  261.8 1.9 constant_dynamic-slice_fusion
  263.6 85.4 %reduce-scatter.5.cloned.1.call-done = f32[128,1664]{1,0:T(8,128)} async-done(((f32[1024,1664]{1,0:T(8,128)}), f32[128,1664]{1,0:T(8,128)}) %reduce-scatter.5.cloned.1.call-update) | async-done | bytes 851984 | tf_op jit(solution)/shard_map/reduce_scatter | solution.py:29
  349.0 105.1 %reduce-scatter.3.cloned.1.call-done = f32[128,1664]{1,0:T(8,128)} async-done(((f32[1024,1664]{1,0:T(8,128)}), f32[128,1664]{1,0:T(8,128)}) %reduce-scatter.3.cloned.1.call-update) | async-done | bytes 851984 | tf_op jit(solution)/shard_map/reduce_scatter | solution.py:28
  454.1 2.5 multiply_multiply_fusion
  (1 shorter events, 0.0 us)
Async XLA Ops:
  7.2 51.7 %copy-start = (bf16[512,2048]{1,0:T(8,128)(2,1)S(1)}, bf16[512,2048]{1,0:T(8,128)(2,1)}, u32[]{:S(2)}) copy-start(bf16[512,2048]{1,0:T(8,128)(2,1)} %param.8) | copy-start | bytes 6291460
  7.2 58.4 %copy-start.1 = (bf16[64,2048]{1,0:T(8,128)(2,1)S(1)}, bf16[64,2048]{1,0:T(8,128)(2,1)}, u32[]{:S(2)}) copy-start(bf16[64,2048]{1,0:T(8,128)(2,1)} %param.7) | copy-start | bytes 786436
  7.2 51.7 %all-gather.2.cloned.1.call-start = ((), (), s32[]{:S(2)}) async-start(), calls=%async_computation.2 | async-start | bytes 1179648 | tf_op jit(solution)/shard_map/all_gather | solution.py:14
  7.9 200.9 %all-reduce.2.cloned.1.call-start = ((), (), s32[]{:S(2)}) async-start(), calls=%async_computation.3 | async-start | bytes 16777216 | tf_op jit(solution)/shard_map/psum | solution.py:21
  67.6 165.7 %copy-start.2 = (f32[2048]{0:T(1024)S(1)}, f32[2048]{0:T(1024)}, u32[]{:S(2)}) copy-start(f32[2048]{0:T(1024)} %param.9) | copy-start | bytes 24580
  67.6 281.4 %reduce-scatter.5.cloned.1.call-start = ((), (), s32[]{:S(2)}) async-start(), calls=%async_computation.5 | async-start | bytes 7667712 | tf_op jit(solution)/shard_map/reduce_scatter | solution.py:29
  247.5 206.6 %reduce-scatter.3.cloned.1.call-start = ((), (), s32[]{:S(2)}) async-start(), calls=%async_computation.4 | async-start | bytes 7667712 | tf_op jit(solution)/shard_map/reduce_scatter | solution.py:28
Sparse Core Ops, SparseCore 0:
  10.4 48.4 all-gather.1
  67.7 141.0 all-reduce.1
  247.6 101.3 reduce-scatter.4
  352.8 101.3 reduce-scatter.2
where the time goes:
time: 464 us; the launch traced here: 463 us
  waiting for transfers between devices  383 us (83%)
  matrix products  35.2 us (8%)
  blocking collectives  20.4 us (4%)
  between operations  13.8 us (3%)
  other arithmetic  8.5 us (2%)
    psum x1, waiting for transfers between devices, on_device(): total = lax.psum(terms + placed, 'wide')  141 us
    reduce_scatter x1, waiting for transfers between devices, on_device(): lax.psum_scatter(gate_part, 'narrow', scatter_dimension=0, tiled=True)  105 us
    reduce_scatter x1, waiting for transfers between devices, on_device(): lax.psum_scatter(up_part, 'narrow', scatter_dimension=0, tiled=True)  85.4 us
    all_gather x1, waiting for transfers between devices, on_device(): gathered = lax.all_gather(heads_output, 'narrow', axis=0, tiled=True)  50.9 us
    psum x1, blocking collectives, on_device(): squares = lax.psum(jnp.sum(total * total, axis=1), 'narrow')  20.4 us
    dot_general x1, matrix products, on_device(): up_part = jnp.dot(normed, up_weight, preferred_element_type=jnp.float32)  14.2 us
    dot_general x1, matrix products, on_device(): gate_part = jnp.dot(normed, gate_weight, preferred_element_type=jnp.float32)  14.2 us
  transfers between devices with their start and end apart: 4, of which 4 were waited for; matrix products, arithmetic and copies ran while one was open for 3% of the time, Pallas kernels for 0%

commit v1 on v0

v1 whole, which is shorter than its diff:
```python
import functools

import jax
import jax.numpy as jnp
from jax import lax
from jax.experimental import pallas as pl
from jax.experimental.pallas import tpu as pltpu
from jax.sharding import PartitionSpec as P

D = 16384
MESH = pl.DeviceIdType.MESH
F32, BF16 = jnp.float32, jnp.bfloat16
CHUNKS = 4
TILE = 256


def body(C, heads_h, rin_h, wo_h, gain_ref, wg_h, wu_h, res_h, hid_h,
         heads, wo, wgu, rin, s2, acc, r2, rx1, rx2, rxd, ry, res, sq, xn,
         sb2, sb1, sbm, own, rz1, rz2, rzd, sy, ryz, hid,
         ld, st, h_s, h_r, c_s, c_r, x_s, x_r, y_s, y_r, q_s, q_r, g_s, g_r, k_s, k_r,
         z_s, z_r, v_s, v_r):
    R = 64 // C
    ff = wgu.shape[1]
    half = ff // 2
    wide = lax.axis_index("wide")
    narrow = lax.axis_index("narrow")
    ylo, x, core = wide // 8, (wide // 2) % 4, wide % 2
    z, yhi = narrow // 2, narrow % 2
    up1, dn1, op2 = (z + 1) % 4, (z + 3) % 4, (z + 2) % 4

    def at(ylo=ylo, x=x, core=core, z=z, yhi=yhi):
        return (ylo * 8 + x * 2 + core, z * 2 + yhi)

    nar = []
    for dz in range(4):
        for dy in range(2):
            if dz or dy:
                nar.append((at(z=(z + dz) % 4, yhi=(yhi + dy) % 2), ((z + 4 - dz) % 4) * 2 + (yhi + dy) % 2))
    wid = []
    for dx in range(4):
        for dy in range(2):
            if dx or dy:
                wid.append((at(x=(x + dx) % 4, ylo=(ylo + dy) % 2), ((ylo + dy) % 2) * 4 + (x + 4 - dx) % 4))
    sib = at(core=1 - core)

    def rcopy(src, dst, ssem, rsem, dev):
        return pltpu.make_async_remote_copy(src_ref=src, dst_ref=dst, send_sem=ssem, recv_sem=rsem,
                                            device_id=dev, device_id_type=MESH)

    sends = []

    def go(cp):
        cp.start()
        sends.append(cp)

    lh = pltpu.make_async_copy(heads_h, heads.at[narrow], ld.at[0])
    lo = pltpu.make_async_copy(wo_h, wo, ld.at[1])
    lr = pltpu.make_async_copy(rin_h, rin, ld.at[2])
    lg = pltpu.make_async_copy(wg_h, wgu.at[:, pl.ds(0, half)], ld.at[3])
    lu = pltpu.make_async_copy(wu_h, wgu.at[:, pl.ds(half, half)], ld.at[4])
    for cp in (lh, lo, lr, lg, lu):
        cp.start()

    bar = pltpu.get_barrier_semaphore()
    peers = [t for t, _ in nar] + [t for t, _ in wid] + [sib]
    for t in peers:
        pl.semaphore_signal(bar, inc=1, device_id=t, device_id_type=MESH)
    pl.semaphore_wait(bar, len(peers))

    lh.wait()
    rows = [pl.ds(c * R, R) for c in range(C)]
    mine = ylo * 4 + x

    def s_heads(c):
        for i, (t, _) in enumerate(nar):
            blk = heads.at[narrow, :, rows[c], :]
            go(rcopy(blk, blk, h_s.at[c, i], h_r.at[c, i], t))

    def s_proj(c):
        for i, (t, src) in enumerate(nar):
            blk = heads.at[src, :, rows[c], :]
            rcopy(blk, blk, h_s.at[c, i], h_r.at[c, i], t).wait_recv()
        if c == 0:
            lo.wait()
        for par, dst in ((1 - core, s2), (core, acc)):
            @pl.loop(0, 2048 // TILE)
            def _(j):
                cols = pl.ds(pl.multiple_of(j * TILE, TILE), TILE)
                a = heads[:, par, rows[c], :].reshape(8 * R, 512)
                p = jnp.dot(a, wo[:, cols], preferred_element_type=F32)
                dst[:, rows[c], cols] = p.reshape(8, R, TILE)
            if dst is s2:
                go(rcopy(s2.at[:, rows[c], :], r2.at[:, rows[c], :], c_s.at[c], c_r.at[c], sib))

    def xsteps(c):
        xp, xm = at(x=(x + 1) % 4), at(x=(x + 3) % 4)
        far, nx, pv = (x + 2) % 4, (x + 1) % 4, (x + 3) % 4
        r = rows[c]
        first = [rcopy(acc.at[far, r, :], rx1.at[0, r, :], x_s.at[c, 0], x_r.at[c, 0], xp),
                 rcopy(acc.at[4 + far, r, :], rx1.at[1, r, :], x_s.at[c, 1], x_r.at[c, 1], xm)]
        direct = [rcopy(acc.at[4 + nx, r, :], rxd.at[1, r, :], x_s.at[c, 2], x_r.at[c, 2], xp),
                  rcopy(acc.at[pv, r, :], rxd.at[0, r, :], x_s.at[c, 3], x_r.at[c, 3], xm)]
        second = [rcopy(rx1.at[0, r, :], rx2.at[0, r, :], x_s.at[c, 4], x_r.at[c, 4], xp),
                  rcopy(rx1.at[1, r, :], rx2.at[1, r, :], x_s.at[c, 5], x_r.at[c, 5], xm)]
        return first, direct, second, (nx, 4 + pv)

    def s_pair(c):
        rcopy(s2.at[:, rows[c], :], r2.at[:, rows[c], :], c_s.at[c], c_r.at[c], sib).wait_recv()

        @pl.loop(0, 8)
        def _(b):
            acc[b, rows[c], :] = acc[b, rows[c], :] + r2[b, rows[c], :]
        first, direct, _, _ = xsteps(c)
        for cp in first + direct:
            go(cp)

    def s_x2(c):
        first, _, second, mid = xsteps(c)
        for h in range(2):
            first[h].wait_recv()
            rx1[h, rows[c], :] = rx1[h, rows[c], :] + acc[mid[h], rows[c], :]
            go(second[h])

    def ycopy(c):
        return rcopy(acc.at[(1 - ylo) * 4 + x, rows[c], :], ry.at[rows[c], :], y_s.at[c], y_r.at[c], at(ylo=1 - ylo))

    def s_x3(c):
        _, direct, second, _ = xsteps(c)
        for cp in direct + second:
            cp.wait_recv()
        r = rows[c]
        for h in (1 - ylo, ylo):
            b = h * 4 + x
            acc[b, r, :] = acc[b, r, :] + rx2[h, r, :] + rxd[h, r, :]
            if h is not ylo:
                go(ycopy(c))

    def s_res(c):
        ycopy(c).wait_recv()
        if c == 0:
            lr.wait()
        r = rows[c]
        total = rin[r, :].astype(F32) + (acc[mine, r, :] + ry[r, :])
        res[r, :] = total
        out = pltpu.make_async_copy(res.at[r, :], res_h.at[r, :], st.at[0, c])
        out.start()
        outs.append(out)
        sq[narrow, r, :] = jnp.broadcast_to(jnp.sum(total * total, axis=1, keepdims=True), (R, 128))
        for i, (t, _) in enumerate(nar):
            blk = sq.at[narrow, r, :]
            go(rcopy(blk, blk, q_s.at[c, i], q_r.at[c, i], t))

    def s_norm(c):
        r = rows[c]
        for i, (t, src) in enumerate(nar):
            blk = sq.at[src, r, :]
            rcopy(blk, blk, q_s.at[c, i], q_r.at[c, i], t).wait_recv()
        ssum = sq[0, r, :]
        for i in range(1, 8):
            ssum = ssum + sq[i, r, :]
        scale = (1.0 / jnp.sqrt(ssum / D + 1e-05))[:, :1]
        xn[mine, core, r, :] = (res[r, :] * scale * gain_ref[...]).astype(BF16)
        blk = xn.at[mine, core, r, :]
        for i, (t, _) in enumerate(wid):
            go(rcopy(blk, blk, g_s.at[c, i], g_r.at[c, i], t))

    def s_gath(c):
        r = rows[c]
        for i, (t, src) in enumerate(wid):
            blk = xn.at[src, core, r, :]
            rcopy(blk, blk, g_s.at[c, i], g_r.at[c, i], t).wait_recv()
        blk = xn.at[:, core, r, :]
        go(rcopy(blk, blk, k_s.at[c], k_r.at[c], sib))

    def zsteps(c):
        zp, zm = at(z=up1), at(z=dn1)
        r = rows[c]
        first = [rcopy(sb2.at[0, :, r, :], rz1.at[0, :, r, :], z_s.at[c, 0], z_r.at[c, 0], zp),
                 rcopy(sb2.at[1, :, r, :], rz1.at[1, :, r, :], z_s.at[c, 1], z_r.at[c, 1], zm)]
        direct = [rcopy(sb1.at[1, :, r, :], rzd.at[1, :, r, :], z_s.at[c, 2], z_r.at[c, 2], zp),
                  rcopy(sbm.at[0, :, r, :], rzd.at[0, :, r, :], z_s.at[c, 3], z_r.at[c, 3], zm)]
        second = [rcopy(rz1.at[0, :, r, :], rz2.at[0, :, r, :], z_s.at[c, 4], z_r.at[c, 4], zp),
                  rcopy(rz1.at[1, :, r, :], rz2.at[1, :, r, :], z_s.at[c, 5], z_r.at[c, 5], zm)]
        return first, direct, second

    def s_mlp(c):
        r = rows[c]
        blk = xn.at[:, 1 - core, r, :]
        rcopy(blk, blk, k_s.at[c], k_r.at[c], sib).wait_recv()
        if c == 0:
            lg.wait()
            lu.wait()

        @pl.loop(0, ff // TILE)
        def _(j):
            cols = pl.ds(pl.multiple_of(j * TILE, TILE), TILE)
            w = wgu[:, cols]
            a = jnp.concatenate(
                [xn[pl.ds(b * 2, 2), :, r, :].reshape(4 * R, 2048) for b in (op2, up1, dn1, z)], axis=0)
            p = jnp.dot(a, w, preferred_element_type=F32).reshape(4, 2, 2, R, TILE)
            sb2[:, :, r, cols] = p[0].astype(BF16)
            sb1[:, :, r, cols] = p[1].astype(BF16)
            sbm[:, :, r, cols] = p[2].astype(BF16)
            own[:, :, r, cols] = p[3]
        first, direct, _ = zsteps(c)
        for cp in first + direct:
            go(cp)

    def s_z2(c):
        first, _, second = zsteps(c)
        for h, part in ((0, sb1), (1, sbm)):
            first[h].wait_recv()
            for j in range(2):
                rz1[h, j, rows[c], :] = (rz1[h, j, rows[c], :].astype(F32)
                                         + part[h, j, rows[c], :].astype(F32)).astype(BF16)
            go(second[h])

    def vcopy(c):
        return rcopy(sy.at[:, rows[c], :], ryz.at[:, rows[c], :], v_s.at[c], v_r.at[c], at(yhi=1 - yhi))

    def s_z3(c):
        _, direct, second = zsteps(c)
        for cp in direct + second:
            cp.wait_recv()
        r = rows[c]
        for j in range(2):
            h = 1 - yhi
            sy[j, r, :] = (own[h, j, r, :] + rz2[h, j, r, :].astype(F32) + rzd[h, j, r, :].astype(F32)).astype(BF16)
        go(vcopy(c))

    def s_out(c):
        vcopy(c).wait_recv()
        r = rows[c]
        for j in range(2):
            def total(cols):
                return (own[yhi, j, r, cols] + rz2[yhi, j, r, cols].astype(F32)
                        + rzd[yhi, j, r, cols].astype(F32) + ryz[j, r, cols].astype(F32))
            g = total(pl.ds(0, half))
            u = total(pl.ds(half, half))
            hid[j, r, :] = g / (1.0 + jnp.exp(-g)) * u
        out = pltpu.make_async_copy(hid.at[:, r, :], hid_h.at[:, r, :], st.at[1, c])
        out.start()
        outs.append(out)

    outs = []
    stage = [s_heads, s_proj, s_pair, s_x2, s_x3, s_res, s_norm, s_gath, s_mlp, s_z2, s_z3, s_out]
    for s, c in SCHEDULE(C, len(stage)):
        stage[s](c)
    for cp in sends:
        cp.wait_send()
    for cp in outs:
        cp.wait()


def SCHEDULE(C, n):
    return [(s, c) for s in range(n) for c in range(C)]


def on_device(heads_output, residual_in, out_weight, norm_gain, gate_weight, up_weight):
    C = CHUNKS
    dm, ffd = gate_weight.shape
    rows = residual_in.shape[0]
    anys = pl.BlockSpec(memory_space=pl.ANY)
    vm = pl.BlockSpec(memory_space=pltpu.VMEM)
    dma = pltpu.SemaphoreType.DMA
    V = pltpu.VMEM
    zb = (2, 2, rows, 2 * ffd)
    res, hid = pl.pallas_call(
        functools.partial(body, C),
        out_shape=(jax.ShapeDtypeStruct((rows, dm), F32), jax.ShapeDtypeStruct((2, rows, ffd), F32)),
        in_specs=[anys, anys, anys, vm, anys, anys],
        out_specs=(anys, anys),
        scratch_shapes=[
            V((8, 2, rows, 512), BF16), V((512, dm), BF16), V((dm, 2 * ffd), BF16), V((rows, dm), BF16),
            V((8, rows, dm), F32), V((8, rows, dm), F32), V((8, rows, dm), F32),
            V((2, rows, dm), F32), V((2, rows, dm), F32), V((2, rows, dm), F32), V((rows, dm), F32),
            V((rows, dm), F32), V((8, rows, 128), F32), V((8, 2, rows, dm), BF16),
            V(zb, BF16), V(zb, BF16), V(zb, BF16), V(zb, F32), V(zb, BF16), V(zb, BF16), V(zb, BF16),
            V((2, rows, 2 * ffd), BF16), V((2, rows, 2 * ffd), BF16), V((2, rows, ffd), F32),
            dma((5,)), dma((2, C)), dma((C, 7)), dma((C, 7)), dma((C,)), dma((C,)), dma((C, 6)), dma((C, 6)),
            dma((C,)), dma((C,)), dma((C, 7)), dma((C, 7)), dma((C, 7)), dma((C, 7)), dma((C,)), dma((C,)),
            dma((C, 6)), dma((C, 6)), dma((C,)), dma((C,)),
        ],
        compiler_params=pltpu.CompilerParams(collective_id=0, has_side_effects=True, vmem_limit_bytes=62 << 20),
        name="layer",
    )(heads_output.reshape(2, rows, 512), residual_in, out_weight, norm_gain.reshape(1, dm), gate_weight, up_weight)
    return res, hid.reshape(2 * rows, ffd)


def solution(mesh):
    return jax.shard_map(
        on_device, mesh=mesh,
        in_specs=(P("narrow", "wide"), P("wide", "narrow"), P("wide", "narrow"), P("narrow"),
                  P("narrow", "wide"), P("narrow", "wide")),
        out_specs=(P("wide", "narrow"), P("narrow", "wide")), check_vma=False)
```

time: 464 us -> 170 us (0.37)
  waiting for transfers between devices: 383 us -> 0 us
  Pallas kernels: 0 us -> 163 us
  matrix products: 35.2 us -> 0 us
  blocking collectives: 20.4 us -> 0 us
  between operations: 13.8 us -> 0.64 us
  other arithmetic: 8.5 us -> 0 us
    reduce_scatter x2 -> x0, waiting for transfers between devices: 190 us -> none  [the longest x1 105 us: on_device(): lax.psum_scatter(gate_part, 'narrow', scatter_dimension=0, tiled=True)]
    pallas_call x0 -> x1, Pallas kernels: none -> 163 us  [on_device(): pl.pallas_call(functools.partial(body, C), out_shape=(jax.ShapeDtypeStruc...]
    psum x1 -> x0, waiting for transfers between devices: 141 us -> none  [on_device(): total = lax.psum(terms + placed, 'wide')]
    all_gather x1 -> x0, waiting for transfers between devices: 50.9 us -> none  [on_device(): gathered = lax.all_gather(heads_output, 'narrow', axis=0, tiled=True)]
    dot_general x3 -> x0, matrix products: 35.2 us -> none  [the longest x1 14.2 us: on_device(): up_part = jnp.dot(normed, up_weight, preferred_element_type=jnp.float32)]
    psum x1 -> x0, blocking collectives: 20.4 us -> none  [on_device(): squares = lax.psum(jnp.sum(total * total, axis=1), 'narrow')]
  transfers between devices with their start and end apart: 4 -> 0, of which waited for: 4 -> 0; matrix products, arithmetic and copies ran while one was open for 3% -> 0% of each run, Pallas kernels for 0% -> 0%
where the time goes in v1:
time: 170 us; the launch traced here: 168 us
  Pallas kernels  163 us (96%)
  local copies, waits for them, and re-layouts  3.98 us (2%)
    pallas_call x1, Pallas kernels, on_device(): pl.pallas_call(functools.partial(body, C), out_shape=(jax.ShapeDtypeStruc...  163 us
    unnamed x2, local copies, waits for them, and re-layouts  3.98 us

profile of v1, /device:TPU:1, one launch (start us, length us, event | category | flops | bytes accessed | tf_op | source)
XLA Modules:
  0.0 167.7 jit_solution(5536779890511500121)
XLA Ops:
  0.6 163.0 %layer.1 = (f32[64,2048]{1,0:T(8,128)}, f32[2,64,1664]{2,1,0:T(8,128)}) custom-call(bf16[2,64,512]{2,1,0:T(8,128)(2,1)} %bitcast.4, bf16[64,2048]{1,0:T(8,128)(2,1)} %rin_h.1, bf16[512,2048]{1,0:T(8,128)(2,1)} %wo_h.1, f32[1,2048]{1,0:T(1,128)} %bitcast.5, bf16[2048,1664]{1,0:T(8,128)(2,1)} %wg_h.1, bf16[2048,1664]{1,0:T(8,128)(2,1)} %wu_h.1), custom_call_target="tpu_custom_call" | custom-call | tf_op jit(solution)/shard_map/layer/pallas_call | solution.py:268
  163.7 1.9 %copy.10 = f32[64,2048]{1,0:T(8,128)} copy(f32[64,2048]{1,0:T(8,128)} %get-tuple-element.8) | data formatting | bytes 1048576
  165.5 2.1 %copy.11 = f32[128,1664]{1,0:T(8,128)} copy(f32[128,1664]{1,0:T(8,128)} %bitcast.3) | data formatting | bytes 1703936

commit v2 on v1

v2 whole, which is shorter than its diff:
```python
import functools

import jax
import jax.numpy as jnp
from jax import lax
from jax.experimental import pallas as pl
from jax.experimental.pallas import tpu as pltpu
from jax.sharding import PartitionSpec as P

D = 16384
MESH = pl.DeviceIdType.MESH
F32, BF16 = jnp.float32, jnp.bfloat16
CHUNKS = 4
PT = 1024
SPLIT = 1


ORDER = [
    (0, 0), (0, 2), (1, 0), (0, 1), (2, 0), (1, 1), (0, 3), (3, 0), (2, 1), (1, 2), (4, 0), (3, 1), (1, 3), (5, 0),
    (2, 2), (6, 0), (4, 1), (7, 0), (3, 2), (5, 1), (8, 0), (2, 3), (4, 2), (6, 1), (9, 0), (10, 0), (7, 1),
    (3, 3), (5, 2), (11, 0), (8, 1), (4, 3), (12, 0), (9, 1), (13, 0), (6, 2), (10, 1), (7, 2), (5, 3), (8, 2),
    (11, 1), (9, 2), (14, 0), (12, 1), (15, 0), (13, 1), (6, 3), (10, 2), (11, 2), (7, 3), (12, 2), (14, 1),
    (8, 3), (9, 3), (13, 2), (15, 1), (10, 3), (14, 2), (16, 0), (11, 3), (17, 0), (15, 2), (12, 3), (13, 3),
    (16, 2), (16, 1), (14, 3), (15, 3), (17, 2), (17, 1), (16, 3), (17, 3),
]


def body(C, heads_h, rin_h, wo_h, gain_ref, wg_h, wu_h, res_h, hid_h,
         heads, wo, wgu, rin, s2, acc, r2, rx1, rx2, rxd, ry, res, sq, xn,
         sb2, sd1, sdm, sp1, spm, own, rz1, rz2, rzd, sy, ryz, hid,
         ld, st, h_s, h_r, c_s, c_r, x_s, x_r, y_s, y_r, q_s, q_r, g_s, g_r, k_s, k_r,
         z_s, z_r, v_s, v_r):
    R = 64 // C
    ff = wgu.shape[1]
    half = ff // 2
    wide = lax.axis_index("wide")
    narrow = lax.axis_index("narrow")
    ylo, x, core = wide // 8, (wide // 2) % 4, wide % 2
    z, yhi = narrow // 2, narrow % 2
    up1, dn1, op2 = (z + 1) % 4, (z + 3) % 4, (z + 2) % 4

    def at(ylo=ylo, x=x, core=core, z=z, yhi=yhi):
        return (ylo * 8 + x * 2 + core, z * 2 + yhi)

    nar = []
    for dz in range(4):
        for dy in range(2):
            if dz or dy:
                nar.append((at(z=(z + dz) % 4, yhi=(yhi + dy) % 2), ((z + 4 - dz) % 4) * 2 + (yhi + dy) % 2))
    sib = at(core=1 - core)

    sends, got = [], set()

    class rcopy:
        def __init__(self, src, dst, sems, idx, dev):
            self.key = (id(sems[0]),) + idx
            self.make = lambda: pltpu.make_async_remote_copy(
                src_ref=src, dst_ref=dst, send_sem=sems[0].at[idx], recv_sem=sems[1].at[idx],
                device_id=dev, device_id_type=MESH)

        def wait_recv(self):
            got.add(self.key)
            self.make().wait_recv()

    def go(cp):
        cp.make().start()
        sends.append(cp)

    lh = pltpu.make_async_copy(heads_h, heads.at[narrow], ld.at[0])
    lo = pltpu.make_async_copy(wo_h, wo, ld.at[1])
    lr = pltpu.make_async_copy(rin_h, rin, ld.at[2])
    cut = half // 256 * 128 + 128
    span = ((0, cut), (cut, half))
    gcols = [pl.ds(2 * a, 2 * (b - a)) for a, b in span]
    lw = []
    for g, (a, b) in enumerate(span):
        lw.append([pltpu.make_async_copy(w.at[:, pl.ds(a, b - a)], wgu.at[:, pl.ds(2 * a + o * (b - a), b - a)],
                                         ld.at[3 + 2 * g + o]) for o, w in enumerate((wg_h, wu_h))])
    for cp in [lh, lo, lr] + lw[0] + lw[1]:
        cp.start()

    bar = pltpu.get_barrier_semaphore()
    peers = [t for t, _ in nar] + [at(x=(x + 1) % 4), at(x=(x + 3) % 4), at(ylo=1 - ylo), sib]
    for t in peers:
        pl.semaphore_signal(bar, inc=1, device_id=t, device_id_type=MESH)
    pl.semaphore_wait(bar, len(peers))

    lh.wait()
    rows = [pl.ds(c * R, R) for c in range(C)]
    mine = ylo * 4 + x

    def s_heads(c):
        for i, (t, _) in enumerate(nar):
            blk = heads.at[narrow, :, rows[c], :]
            go(rcopy(blk, blk, (h_s, h_r), (c, i,), t))

    def s_proj(c):
        for i, (t, src) in enumerate(nar):
            blk = heads.at[src, :, rows[c], :]
            rcopy(blk, blk, (h_s, h_r), (c, i,), t).wait_recv()
        if c == 0:
            lo.wait()

        @pl.loop(0, 2048 // PT)
        def _(j):
            cols = pl.ds(pl.multiple_of(j * PT, PT), PT)
            a = jnp.concatenate([heads[:, p, rows[c], :].reshape(8 * R, 512) for p in (1 - core, core)], axis=0)
            p = jnp.dot(a, wo[:, cols], preferred_element_type=F32)
            s2[:, rows[c], cols] = p[:8 * R].reshape(8, R, PT)
            acc[:, rows[c], cols] = p[8 * R:].reshape(8, R, PT)
        go(rcopy(s2.at[:, rows[c], :], r2.at[:, rows[c], :], (c_s, c_r), (c,), sib))

    def xsteps(c):
        xp, xm = at(x=(x + 1) % 4), at(x=(x + 3) % 4)
        far, nx, pv = (x + 2) % 4, (x + 1) % 4, (x + 3) % 4
        r = rows[c]
        first = [rcopy(acc.at[far, r, :], rx1.at[0, r, :], (x_s, x_r), (c, 0,), xp),
                 rcopy(acc.at[4 + far, r, :], rx1.at[1, r, :], (x_s, x_r), (c, 1,), xm)]
        direct = [rcopy(acc.at[4 + nx, r, :], rxd.at[1, r, :], (x_s, x_r), (c, 2,), xp),
                  rcopy(acc.at[pv, r, :], rxd.at[0, r, :], (x_s, x_r), (c, 3,), xm)]
        second = [rcopy(rx1.at[0, r, :], rx2.at[0, r, :], (x_s, x_r), (c, 4,), xp),
                  rcopy(rx1.at[1, r, :], rx2.at[1, r, :], (x_s, x_r), (c, 5,), xm)]
        return first, direct, second, (nx, 4 + pv)

    def s_pair(c):
        rcopy(s2.at[:, rows[c], :], r2.at[:, rows[c], :], (c_s, c_r), (c,), sib).wait_recv()

        @pl.loop(0, 8)
        def _(b):
            acc[b, rows[c], :] = acc[b, rows[c], :] + r2[b, rows[c], :]
        first, direct, _, _ = xsteps(c)
        for cp in first + direct:
            go(cp)

    def s_x2(c):
        first, _, second, mid = xsteps(c)
        for h in range(2):
            first[h].wait_recv()
            rx1[h, rows[c], :] = rx1[h, rows[c], :] + acc[mid[h], rows[c], :]
            go(second[h])

    def ycopy(c):
        return rcopy(acc.at[(1 - ylo) * 4 + x, rows[c], :], ry.at[rows[c], :], (y_s, y_r), (c,), at(ylo=1 - ylo))

    def s_x3(c):
        _, direct, second, _ = xsteps(c)
        for cp in direct + second:
            cp.wait_recv()
        r = rows[c]
        for h in (1 - ylo, ylo):
            b = h * 4 + x
            acc[b, r, :] = acc[b, r, :] + rx2[h, r, :] + rxd[h, r, :]
            if h is not ylo:
                go(ycopy(c))

    def s_res(c):
        ycopy(c).wait_recv()
        if c == 0:
            lr.wait()
        r = rows[c]
        total = rin[r, :].astype(F32) + (acc[mine, r, :] + ry[r, :])
        res[r, :] = total
        out = pltpu.make_async_copy(res.at[r, :], res_h.at[r, :], st.at[0, c])
        out.start()
        outs.append(out)
        sq[narrow, r, :] = jnp.broadcast_to(jnp.sum(total * total, axis=1, keepdims=True), (R, 128))
        for i, (t, _) in enumerate(nar):
            blk = sq.at[narrow, r, :]
            go(rcopy(blk, blk, (q_s, q_r), (c, i,), t))

    def s_norm(c):
        r = rows[c]
        for i, (t, src) in enumerate(nar):
            blk = sq.at[src, r, :]
            rcopy(blk, blk, (q_s, q_r), (c, i,), t).wait_recv()
        ssum = sq[0, r, :]
        for i in range(1, 8):
            ssum = ssum + sq[i, r, :]
        scale = (1.0 / jnp.sqrt(ssum / D + 1e-05))[:, :1]
        xn[mine, core, r, :] = (res[r, :] * scale * gain_ref[...]).astype(BF16)
        for i, t in ((0, xp), (1, xm), (2, yp)):
            go(gcopy(c, mine, i, t))
        go(kcopy(c, 0, mine))

    xp, xm, yp = at(x=(x + 1) % 4), at(x=(x + 3) % 4), at(ylo=1 - ylo)
    yours = (1 - ylo) * 4 + x

    def gcopy(c, b, i, t):
        blk = xn.at[b, core, rows[c], :]
        return rcopy(blk, blk, (g_s, g_r), (c, i), t)

    def kcopy(c, i, b):
        blk = xn.at[b, core, rows[c], :]
        return rcopy(blk, blk, (k_s, k_r), (c, i), sib)

    pvx, nxx, far = (x + 3) % 4, (x + 1) % 4, (x + 2) % 4
    held = [mine, ylo * 4 + pvx, ylo * 4 + nxx, yours, (1 - ylo) * 4 + pvx, (1 - ylo) * 4 + nxx, far, 4 + far]

    def s_g2(c):
        gcopy(c, yours, 2, yp).wait_recv()
        go(gcopy(c, yours, 3, xp))
        go(gcopy(c, yours, 4, xm))
        go(kcopy(c, 3, yours))

    def s_g3(c):
        gcopy(c, held[1], 0, xp).wait_recv()
        gcopy(c, held[2], 1, xm).wait_recv()
        gcopy(c, held[4], 3, xp).wait_recv()
        gcopy(c, held[5], 4, xm).wait_recv()
        go(gcopy(c, pvx, 5, xp))
        go(gcopy(c, 4 + nxx, 6, xm))
        for k in (1, 2, 4, 5):
            go(kcopy(c, k, held[k]))

    def s_gath(c):
        gcopy(c, far, 5, xp).wait_recv()
        gcopy(c, 4 + far, 6, xm).wait_recv()
        for k in (6, 7):
            go(kcopy(c, k, held[k]))

    zp, zm = at(z=up1), at(z=dn1)

    def zsteps(c, g):
        r, w = rows[c], gcols[g]

        def cp(src, dst, i, t):
            return rcopy(src, dst, (z_s, z_r), (c, g, i), t)
        first = [cp(sb2.at[0, :, r, w], rz1.at[0, :, r, w], 0, zp), cp(sb2.at[1, :, r, w], rz1.at[1, :, r, w], 1, zm)]
        direct = [cp(sdm.at[:, r, w], rzd.at[0, :, r, w], 3, zm), cp(sd1.at[:, r, w], rzd.at[1, :, r, w], 2, zp)]
        second = [cp(rz1.at[0, :, r, w], rz2.at[0, :, r, w], 4, zp), cp(rz1.at[1, :, r, w], rz2.at[1, :, r, w], 5, zm)]
        return first, direct, second

    def mlp(c, g):
        r = rows[c]
        if g == 0:
            for k in range(8):
                blk = xn.at[held[k], 1 - core, r, :]
                rcopy(blk, blk, (k_s, k_r), (c, k), sib).wait_recv()
        if c == 0:
            for cp in lw[g]:
                cp.wait()
        base, tile = 2 * span[g][0], 2 * (span[g][1] - span[g][0]) // SPLIT

        @pl.loop(0, SPLIT)
        def _(j):
            cols = pl.ds(pl.multiple_of(base + j * tile, 128), tile)
            a = jnp.concatenate(
                [xn[pl.ds(b * 2, 2), :, r, :].reshape(4 * R, 2048) for b in (op2, up1, dn1, z)], axis=0)
            p = jnp.dot(a, wgu[:, cols], preferred_element_type=F32).reshape(4, 2, 2, R, tile)
            sb2[:, :, r, cols] = p[0].astype(BF16)
            sp1[:, r, cols] = p[1, 0]
            sd1[:, r, cols] = p[1, 1].astype(BF16)
            sdm[:, r, cols] = p[2, 0].astype(BF16)
            spm[:, r, cols] = p[2, 1]
            own[:, :, r, cols] = p[3]
        first, direct, _ = zsteps(c, g)
        for cp in first + direct:
            go(cp)

    def z2(c, g):
        first, _, second = zsteps(c, g)
        r, w = rows[c], gcols[g]
        for h, part in ((0, sp1), (1, spm)):
            first[h].wait_recv()
            for j in range(2):
                rz1[h, j, r, w] = (rz1[h, j, r, w].astype(F32) + part[j, r, w]).astype(BF16)
            go(second[h])

    def vcopy(c, g):
        return rcopy(sy.at[:, rows[c], gcols[g]], ryz.at[:, rows[c], gcols[g]], (v_s, v_r), (c, g), at(yhi=1 - yhi))

    def z3(c, g):
        _, direct, second = zsteps(c, g)
        for cp in direct + second:
            cp.wait_recv()
        r, w, h = rows[c], gcols[g], 1 - yhi
        for j in range(2):
            sy[j, r, w] = (own[h, j, r, w] + rz2[h, j, r, w].astype(F32) + rzd[h, j, r, w].astype(F32)).astype(BF16)
        go(vcopy(c, g))

    def out(c, g):
        vcopy(c, g).wait_recv()
        r, (a, b) = rows[c], span[g]
        for j in range(2):
            def total(o):
                w = pl.ds(2 * a + o * (b - a), b - a)
                return (own[yhi, j, r, w] + rz2[yhi, j, r, w].astype(F32)
                        + rzd[yhi, j, r, w].astype(F32) + ryz[j, r, w].astype(F32))
            v, u = total(0), total(1)
            hid[j, r, pl.ds(a, b - a)] = v / (1.0 + jnp.exp(-v)) * u
        cp = pltpu.make_async_copy(hid.at[:, r, pl.ds(a, b - a)], hid_h.at[:, r, pl.ds(a, b - a)], st.at[1 + g, c])
        cp.start()
        outs.append(cp)

    outs = []
    def grouped(f):
        return [functools.partial(f, g=0), functools.partial(f, g=1)]
    stage = [s_heads, s_proj, s_pair, s_x2, s_x3, s_res, s_norm, s_g2, s_g3, s_gath,
             *grouped(mlp), *grouped(z2), *grouped(z3), *grouped(out)]
    for s, c in ORDER:
        stage[s](c)
    for cp in sends:
        cp.make().wait_send()
    for cp in outs:
        cp.wait()


def on_device(heads_output, residual_in, out_weight, norm_gain, gate_weight, up_weight):
    C = CHUNKS
    dm, ffd = gate_weight.shape
    rows = residual_in.shape[0]
    anys = pl.BlockSpec(memory_space=pl.ANY)
    vm = pl.BlockSpec(memory_space=pltpu.VMEM)
    dma = pltpu.SemaphoreType.DMA
    V = pltpu.VMEM
    zb, zh = (2, 2, rows, 2 * ffd), (2, rows, 2 * ffd)
    res, hid = pl.pallas_call(
        functools.partial(body, C),
        out_shape=(jax.ShapeDtypeStruct((rows, dm), F32), jax.ShapeDtypeStruct((2, rows, ffd), F32)),
        in_specs=[anys, anys, anys, vm, anys, anys],
        out_specs=(anys, anys),
        scratch_shapes=[
            V((8, 2, rows, 512), BF16), V((512, dm), BF16), V((dm, 2 * ffd), BF16), V((rows, dm), BF16),
            V((8, rows, dm), F32), V((8, rows, dm), F32), V((8, rows, dm), F32),
            V((2, rows, dm), F32), V((2, rows, dm), F32), V((2, rows, dm), F32), V((rows, dm), F32),
            V((rows, dm), F32), V((8, rows, 128), F32), V((8, 2, rows, dm), BF16),
            V(zb, BF16), V(zh, BF16), V(zh, BF16), V(zh, F32), V(zh, F32), V(zb, F32), V(zb, BF16), V(zb, BF16), V(zb, BF16),
            V((2, rows, 2 * ffd), BF16), V((2, rows, 2 * ffd), BF16), V((2, rows, ffd), F32),
            dma((7,)), dma((3, C)), dma((C, 7)), dma((C, 7)), dma((C,)), dma((C,)), dma((C, 6)), dma((C, 6)),
            dma((C,)), dma((C,)), dma((C, 7)), dma((C, 7)), dma((C, 7)), dma((C, 7)), dma((C, 8)), dma((C, 8)),
            dma((C, 2, 6)), dma((C, 2, 6)), dma((C, 2)), dma((C, 2)),
        ],
        compiler_params=pltpu.CompilerParams(collective_id=0, has_side_effects=True, vmem_limit_bytes=62 << 20),
        name="layer",
    )(heads_output.reshape(2, rows, 512), residual_in, out_weight, norm_gain.reshape(1, dm), gate_weight, up_weight)
    return res, hid.reshape(2 * rows, ffd)


def solution(mesh):
    return jax.shard_map(
        on_device, mesh=mesh,
        in_specs=(P("narrow", "wide"), P("wide", "narrow"), P("wide", "narrow"), P("narrow"),
                  P("narrow", "wide"), P("narrow", "wide")),
        out_specs=(P("wide", "narrow"), P("narrow", "wide")), check_vma=False)
```

time: 170 us -> 128 us (0.75); the launches traced: 168 us -> 127 us
  Pallas kernels: 163 us -> 123 us
    pallas_call x1, Pallas kernels: 163 us -> 123 us  [on_device(): pl.pallas_call(functools.partial(body, C), out_shape=(jax.ShapeDtypeStruc...]
where the time goes in v2:
time: 128 us; the launch traced here: 127 us
  Pallas kernels  123 us (96%)
  local copies, waits for them, and re-layouts  3.98 us (3%)
    pallas_call x1, Pallas kernels, on_device(): pl.pallas_call(functools.partial(body, C), out_shape=(jax.ShapeDtypeStruc...  123 us
    unnamed x2, local copies, waits for them, and re-layouts  3.98 us

profile of v2, /device:TPU:1, one launch (start us, length us, event | category | flops | bytes accessed | tf_op | source)
XLA Modules:
  0.0 127.4 jit_solution(11275573146354941245)
XLA Ops:
  0.6 122.8 %layer.1 = (f32[64,2048]{1,0:T(8,128)}, f32[2,64,1664]{2,1,0:T(8,128)}) custom-call(bf16[2,64,512]{2,1,0:T(8,128)(2,1)} %bitcast.4, bf16[64,2048]{1,0:T(8,128)(2,1)} %rin_h.1, bf16[512,2048]{1,0:T(8,128)(2,1)} %wo_h.1, f32[1,2048]{1,0:T(1,128)} %bitcast.5, bf16[2048,1664]{1,0:T(8,128)(2,1)} %wg_h.1, bf16[2048,1664]{1,0:T(8,128)(2,1)} %wu_h.1), custom_call_target="tpu_custom_call" | custom-call | tf_op jit(solution)/shard_map/layer/pallas_call | solution.py:317
  123.4 1.9 %copy.10 = f32[64,2048]{1,0:T(8,128)} copy(f32[64,2048]{1,0:T(8,128)} %get-tuple-element.8) | data formatting | bytes 1048576
  125.3 2.1 %copy.11 = f32[128,1664]{1,0:T(8,128)} copy(f32[128,1664]{1,0:T(8,128)} %bitcast.3) | data formatting | bytes 1703936

commit v3 on v2

--- a/solution.py
+++ b/solution.py
@@ -10,18 +10,23 @@
 D = 16384
 MESH = pl.DeviceIdType.MESH
 F32, BF16 = jnp.float32, jnp.bfloat16
-CHUNKS = 4
+SIZES = (8, 8, 16, 16, 8, 8)
+DIRECT = (True, False, False, False, False, False)
 PT = 1024
 SPLIT = 1
+HAND = 2
 
 
 ORDER = [
-    (0, 0), (0, 2), (1, 0), (0, 1), (2, 0), (1, 1), (0, 3), (3, 0), (2, 1), (1, 2), (4, 0), (3, 1), (1, 3), (5, 0),
-    (2, 2), (6, 0), (4, 1), (7, 0), (3, 2), (5, 1), (8, 0), (2, 3), (4, 2), (6, 1), (9, 0), (10, 0), (7, 1),
-    (3, 3), (5, 2), (11, 0), (8, 1), (4, 3), (12, 0), (9, 1), (13, 0), (6, 2), (10, 1), (7, 2), (5, 3), (8, 2),
-    (11, 1), (9, 2), (14, 0), (12, 1), (15, 0), (13, 1), (6, 3), (10, 2), (11, 2), (7, 3), (12, 2), (14, 1),
-    (8, 3), (9, 3), (13, 2), (15, 1), (10, 3), (14, 2), (16, 0), (11, 3), (17, 0), (15, 2), (12, 3), (13, 3),
-    (16, 2), (16, 1), (14, 3), (15, 3), (17, 2), (17, 1), (16, 3), (17, 3),
+    (0, 0), (0, 1), (0, 2), (1, 0), (2, 0), (1, 1), (1, 2), (2, 1), (0, 5), (3, 0), (0, 3), (3, 1), (2, 2), (4, 0),
+    (1, 3), (5, 0), (3, 2), (2, 3), (4, 1), (0, 4), (6, 0), (1, 5), (5, 1), (4, 2), (1, 4), (7, 0), (6, 1), (3, 3),
+    (5, 2), (7, 1), (8, 0), (2, 4), (9, 0), (6, 2), (4, 3), (8, 1), (10, 0), (7, 2), (2, 5), (11, 0), (9, 1),
+    (3, 4), (5, 3), (12, 0), (8, 2), (10, 1), (13, 0), (6, 3), (11, 1), (3, 5), (9, 2), (4, 4), (12, 1), (7, 3),
+    (10, 2), (5, 4), (8, 3), (4, 5), (13, 1), (14, 0), (11, 2), (9, 3), (5, 5), (6, 4), (12, 2), (10, 3), (7, 4),
+    (13, 2), (11, 3), (6, 5), (8, 4), (7, 5), (15, 0), (9, 4), (10, 4), (12, 3), (13, 3), (14, 2), (16, 0), (8, 5),
+    (17, 0), (11, 4), (15, 2), (12, 4), (9, 5), (14, 1), (10, 5), (14, 3), (16, 2), (11, 5), (17, 2), (15, 1),
+    (13, 4), (12, 5), (16, 1), (14, 4), (15, 3), (16, 3), (13, 5), (15, 4), (17, 1), (14, 5), (16, 4), (15, 5),
+    (17, 4), (16, 5), (17, 3), (17, 5),
 ]
 
 
@@ -30,7 +35,6 @@
          sb2, sd1, sdm, sp1, spm, own, rz1, rz2, rzd, sy, ryz, hid,
          ld, st, h_s, h_r, c_s, c_r, x_s, x_r, y_s, y_r, q_s, q_r, g_s, g_r, k_s, k_r,
          z_s, z_r, v_s, v_r):
-    R = 64 // C
     ff = wgu.shape[1]
     half = ff // 2
     wide = lax.axis_index("wide")
@@ -52,10 +56,10 @@
     sends, got = [], set()
 
     class rcopy:
-        def __init__(self, src, dst, sems, idx, dev):
+        def __init__(self, src, dst, sems, idx, dev, ridx=None):
             self.key = (id(sems[0]),) + idx
             self.make = lambda: pltpu.make_async_remote_copy(
-                src_ref=src, dst_ref=dst, send_sem=sems[0].at[idx], recv_sem=sems[1].at[idx],
+                src_ref=src, dst_ref=dst, send_sem=sems[0].at[idx], recv_sem=sems[1].at[idx if ridx is None else ridx],
                 device_id=dev, device_id_type=MESH)
 
         def wait_recv(self):
@@ -76,17 +80,17 @@
     for g, (a, b) in enumerate(span):
         lw.append([pltpu.make_async_copy(w.at[:, pl.ds(a, b - a)], wgu.at[:, pl.ds(2 * a + o * (b - a), b - a)],
                                          ld.at[3 + 2 * g + o]) for o, w in enumerate((wg_h, wu_h))])
-    for cp in [lh, lo, lr] + lw[0] + lw[1]:
+    for cp in [lh, lo]:
         cp.start()
 
     bar = pltpu.get_barrier_semaphore()
-    peers = [t for t, _ in nar] + [at(x=(x + 1) % 4), at(x=(x + 3) % 4), at(ylo=1 - ylo), sib]
+    peers = [t for t, _ in nar] + [at(x=(x + dx) % 4, ylo=yy) for dx in (1, 2, 3) for yy in (ylo, 1 - ylo)] + [at(ylo=1 - ylo), sib]
     for t in peers:
         pl.semaphore_signal(bar, inc=1, device_id=t, device_id_type=MESH)
     pl.semaphore_wait(bar, len(peers))
 
     lh.wait()
-    rows = [pl.ds(c * R, R) for c in range(C)]
+    rows = [pl.ds(sum(SIZES[:c]), SIZES[c]) for c in range(C)]
     mine = ylo * 4 + x
 
     def s_heads(c):
@@ -100,14 +104,16 @@
             rcopy(blk, blk, (h_s, h_r), (c, i,), t).wait_recv()
         if c == 0:
             lo.wait()
+            for cp in [lr] + lw[0] + lw[1]:
+                cp.start()
 
         @pl.loop(0, 2048 // PT)
         def _(j):
             cols = pl.ds(pl.multiple_of(j * PT, PT), PT)
-            a = jnp.concatenate([heads[:, p, rows[c], :].reshape(8 * R, 512) for p in (1 - core, core)], axis=0)
+            a = jnp.concatenate([heads[:, p, rows[c], :].reshape(8 * SIZES[c], 512) for p in (1 - core, core)], axis=0)
             p = jnp.dot(a, wo[:, cols], preferred_element_type=F32)
-            s2[:, rows[c], cols] = p[:8 * R].reshape(8, R, PT)
-            acc[:, rows[c], cols] = p[8 * R:].reshape(8, R, PT)
+            s2[:, rows[c], cols] = p[:8 * SIZES[c]].reshape(8, SIZES[c], PT)
+            acc[:, rows[c], cols] = p[8 * SIZES[c]:].reshape(8, SIZES[c], PT)
         go(rcopy(s2.at[:, rows[c], :], r2.at[:, rows[c], :], (c_s, c_r), (c,), sib))
 
     def xsteps(c):
@@ -163,7 +169,7 @@
         out = pltpu.make_async_copy(res.at[r, :], res_h.at[r, :], st.at[0, c])
         out.start()
         outs.append(out)
-        sq[narrow, r, :] = jnp.broadcast_to(jnp.sum(total * total, axis=1, keepdims=True), (R, 128))
+        sq[narrow, r, :] = jnp.broadcast_to(jnp.sum(total * total, axis=1, keepdims=True), (SIZES[c], 128))
         for i, (t, _) in enumerate(nar):
             blk = sq.at[narrow, r, :]
             go(rcopy(blk, blk, (q_s, q_r), (c, i,), t))
@@ -180,14 +186,19 @@
         xn[mine, core, r, :] = (res[r, :] * scale * gain_ref[...]).astype(BF16)
         for i, t in ((0, xp), (1, xm), (2, yp)):
             go(gcopy(c, mine, i, t))
+        if DIRECT[c]:
+            other = 1 - ylo
+            for i, ri, t in ((3, 3, at(x=nxx, ylo=other)), (4, 4, at(x=pvx, ylo=other)),
+                             (5, 5 + ylo, at(x=far)), (6, 5 + ylo, at(x=far, ylo=other))):
+                go(gcopy(c, mine, i, t, ri))
         go(kcopy(c, 0, mine))
 
     xp, xm, yp = at(x=(x + 1) % 4), at(x=(x + 3) % 4), at(ylo=1 - ylo)
     yours = (1 - ylo) * 4 + x
 
-    def gcopy(c, b, i, t):
+    def gcopy(c, b, i, t, ri=None):
         blk = xn.at[b, core, rows[c], :]
-        return rcopy(blk, blk, (g_s, g_r), (c, i), t)
+        return rcopy(blk, blk, (g_s, g_r), (c, i), t, None if ri is None else (c, ri))
 
     def kcopy(c, i, b):
         blk = xn.at[b, core, rows[c], :]
@@ -198,8 +209,9 @@
 
     def s_g2(c):
         gcopy(c, yours, 2, yp).wait_recv()
-        go(gcopy(c, yours, 3, xp))
-        go(gcopy(c, yours, 4, xm))
+        if not DIRECT[c]:
+            go(gcopy(c, yours, 3, xp))
+            go(gcopy(c, yours, 4, xm))
         go(kcopy(c, 3, yours))
 
     def s_g3(c):
@@ -207,8 +219,9 @@
         gcopy(c, held[2], 1, xm).wait_recv()
         gcopy(c, held[4], 3, xp).wait_recv()
         gcopy(c, held[5], 4, xm).wait_recv()
-        go(gcopy(c, pvx, 5, xp))
-        go(gcopy(c, 4 + nxx, 6, xm))
+        if not DIRECT[c]:
+            go(gcopy(c, pvx, 5, xp))
+            go(gcopy(c, 4 + nxx, 6, xm))
         for k in (1, 2, 4, 5):
             go(kcopy(c, k, held[k]))
 
@@ -231,7 +244,7 @@
         return first, direct, second
 
     def mlp(c, g):
-        r = rows[c]
+        r, R = rows[c], SIZES[c]
         if g == 0:
             for k in range(8):
                 blk = xn.at[held[k], 1 - core, r, :]
@@ -305,8 +318,24 @@
         cp.wait()
 
 
+def handover(res_h, hid_h, res_o, hid_o, res_v, hid_v, sem):
+    def moves(way, src, dst, k):
+        n = src.shape[0] // HAND
+        return [pltpu.make_async_copy(src.at[pl.ds(i * n, n)], dst.at[pl.ds(i * n, n)], sem.at[way, k, i])
+                for i in range(HAND)]
+    into = moves(0, res_h, res_v, 0) + moves(0, hid_h, hid_v, 1)
+    back = moves(1, res_v, res_o, 0) + moves(1, hid_v, hid_o, 1)
+    for cp in into:
+        cp.start()
+    for cp, nx in zip(into, back):
+        cp.wait()
+        nx.start()
+    for cp in back:
+        cp.wait()
+
+
 def on_device(heads_output, residual_in, out_weight, norm_gain, gate_weight, up_weight):
-    C = CHUNKS
+    C = len(SIZES)
     dm, ffd = gate_weight.shape
     rows = residual_in.shape[0]
     anys = pl.BlockSpec(memory_space=pl.ANY)
@@ -333,7 +362,11 @@
         compiler_params=pltpu.CompilerParams(collective_id=0, has_side_effects=True, vmem_limit_bytes=62 << 20),
         name="layer",
     )(heads_output.reshape(2, rows, 512), residual_in, out_weight, norm_gain.reshape(1, dm), gate_weight, up_weight)
-    return res, hid.reshape(2 * rows, ffd)
+    out = (jax.ShapeDtypeStruct(res.shape, F32), jax.ShapeDtypeStruct((2 * rows, ffd), F32))
+    return pl.pallas_call(
+        handover, out_shape=out, in_specs=[anys, anys], out_specs=(anys, anys),
+        scratch_shapes=[V(res.shape, F32), V((2 * rows, ffd), F32), dma((2, 2, HAND))], name="handover",
+    )(res, hid.reshape(2 * rows, ffd))
 
 
 def solution(mesh):

time: 128 us -> 124 us (0.969)
  local copies, waits for them, and re-layouts: 3.98 us -> 0 us
    unnamed x2 -> x0, local copies, waits for them, and re-layouts: 3.98 us -> none
    pallas_call x1, Pallas kernels: 123 us -> 120 us  [on_device(): pl.pallas_call(functools.partial(body, C), out_shape=(jax.ShapeDtypeStruc...]
    pallas_call x0 -> x1, Pallas kernels: none -> 2.13 us  [on_device(): pl.pallas_call(handover, out_shape=out, in_specs=[anys, anys], out_specs=...]
where the time goes in v3:
time: 124 us; the launch traced here: 123 us
  Pallas kernels  123 us (99%)
    pallas_call x1, Pallas kernels, on_device(): pl.pallas_call(functools.partial(body, C), out_shape=(jax.ShapeDtypeStruc...  120 us

profile of v3, /device:TPU:1, one launch (start us, length us, event | category | flops | bytes accessed | tf_op | source)
XLA Modules:
  0.0 123.4 jit_solution(8620503685472145370)
XLA Ops:
  0.6 120.5 %layer.1 = (f32[64,2048]{1,0:T(8,128)}, f32[2,64,1664]{2,1,0:T(8,128)}) custom-call(bf16[2,64,512]{2,1,0:T(8,128)(2,1)} %bitcast.4, bf16[64,2048]{1,0:T(8,128)(2,1)} %rin_h.1, bf16[512,2048]{1,0:T(8,128)(2,1)} %wo_h.1, f32[1,2048]{1,0:T(1,128)} %bitcast.5, bf16[2048,1664]{1,0:T(8,128)(2,1)} %wg_h.1, bf16[2048,1664]{1,0:T(8,128)(2,1)} %wu_h.1), custom_call_target="tpu_custom_call" | custom-call | tf_op jit(solution)/shard_map/layer/pallas_call | solution.py:346
  121.1 2.1 %handover.1 = (f32[64,2048]{1,0:T(8,128)}, f32[128,1664]{1,0:T(8,128)}) custom-call(f32[64,2048]{1,0:T(8,128)} %get-tuple-element.4.res_h, f32[128,1664]{1,0:T(8,128)} %bitcast.3), custom_call_target="tpu_custom_call" | custom-call | tf_op jit(solution)/shard_map/handover/pallas_call | solution.py:366

commit v4 on v3

--- a/solution.py
+++ b/solution.py
@@ -18,15 +18,15 @@
 
 
 ORDER = [
-    (0, 0), (0, 1), (0, 2), (1, 0), (2, 0), (1, 1), (1, 2), (2, 1), (0, 5), (3, 0), (0, 3), (3, 1), (2, 2), (4, 0),
-    (1, 3), (5, 0), (3, 2), (2, 3), (4, 1), (0, 4), (6, 0), (1, 5), (5, 1), (4, 2), (1, 4), (7, 0), (6, 1), (3, 3),
-    (5, 2), (7, 1), (8, 0), (2, 4), (9, 0), (6, 2), (4, 3), (8, 1), (10, 0), (7, 2), (2, 5), (11, 0), (9, 1),
-    (3, 4), (5, 3), (12, 0), (8, 2), (10, 1), (13, 0), (6, 3), (11, 1), (3, 5), (9, 2), (4, 4), (12, 1), (7, 3),
-    (10, 2), (5, 4), (8, 3), (4, 5), (13, 1), (14, 0), (11, 2), (9, 3), (5, 5), (6, 4), (12, 2), (10, 3), (7, 4),
-    (13, 2), (11, 3), (6, 5), (8, 4), (7, 5), (15, 0), (9, 4), (10, 4), (12, 3), (13, 3), (14, 2), (16, 0), (8, 5),
-    (17, 0), (11, 4), (15, 2), (12, 4), (9, 5), (14, 1), (10, 5), (14, 3), (16, 2), (11, 5), (17, 2), (15, 1),
-    (13, 4), (12, 5), (16, 1), (14, 4), (15, 3), (16, 3), (13, 5), (15, 4), (17, 1), (14, 5), (16, 4), (15, 5),
-    (17, 4), (16, 5), (17, 3), (17, 5),
+    (0, 0), (0, 1), (0, 2), (0, 3), (1, 0), (1, 1), (0, 5), (2, 0), (2, 1), (3, 0), (1, 2), (3, 1), (0, 4), (2, 2),
+    (4, 1), (4, 0), (1, 3), (3, 2), (2, 3), (5, 1), (5, 0), (1, 4), (6, 1), (4, 2), (3, 3), (7, 1), (1, 5), (8, 1),
+    (6, 0), (5, 2), (4, 3), (9, 1), (2, 4), (6, 2), (10, 1), (7, 0), (8, 0), (11, 1), (9, 0), (3, 4), (5, 3),
+    (10, 0), (7, 2), (8, 2), (2, 5), (11, 0), (6, 3), (4, 4), (12, 1), (9, 2), (12, 0), (3, 5), (13, 0), (13, 1),
+    (10, 2), (7, 3), (8, 3), (5, 4), (11, 2), (4, 5), (12, 2), (14, 1), (9, 3), (5, 5), (13, 2), (6, 4), (10, 3),
+    (14, 0), (11, 3), (14, 2), (7, 4), (8, 4), (6, 5), (9, 4), (7, 5), (8, 5), (12, 3), (15, 2), (15, 0), (13, 3),
+    (16, 2), (9, 5), (10, 4), (15, 1), (10, 5), (14, 3), (11, 5), (12, 5), (11, 4), (16, 1), (12, 4), (17, 1),
+    (15, 3), (13, 5), (13, 4), (14, 5), (14, 4), (15, 5), (16, 3), (15, 4), (16, 0), (16, 5), (17, 3), (16, 4),
+    (17, 0), (17, 2), (17, 5), (17, 4),
 ]
 
 
@@ -53,7 +53,12 @@
                 nar.append((at(z=(z + dz) % 4, yhi=(yhi + dy) % 2), ((z + 4 - dz) % 4) * 2 + (yhi + dy) % 2))
     sib = at(core=1 - core)
 
-    sends, got = [], set()
+    sends, got, met = [], set(), set()
+
+    def first_time(s):
+        new = s not in met
+        met.add(s)
+        return new
 
     class rcopy:
         def __init__(self, src, dst, sems, idx, dev, ridx=None):
@@ -102,7 +107,7 @@
         for i, (t, src) in enumerate(nar):
             blk = heads.at[src, :, rows[c], :]
             rcopy(blk, blk, (h_s, h_r), (c, i,), t).wait_recv()
-        if c == 0:
+        if first_time(1):
             lo.wait()
             for cp in [lr] + lw[0] + lw[1]:
                 cp.start()
@@ -161,10 +166,11 @@
 
     def s_res(c):
         ycopy(c).wait_recv()
-        if c == 0:
+        if first_time(5):
             lr.wait()
         r = rows[c]
-        total = rin[r, :].astype(F32) + (acc[mine, r, :] + ry[r, :])
+        total = acc[mine, r, :] + ry[r, :]
+        total = rin[r, :].astype(F32) + total
         res[r, :] = total
         out = pltpu.make_async_copy(res.at[r, :], res_h.at[r, :], st.at[0, c])
         out.start()
@@ -186,11 +192,12 @@
         xn[mine, core, r, :] = (res[r, :] * scale * gain_ref[...]).astype(BF16)
         for i, t in ((0, xp), (1, xm), (2, yp)):
             go(gcopy(c, mine, i, t))
+        other = 1 - ylo
+        go(gcopy(c, mine, 3, at(x=nxx, ylo=other)))
+        go(gcopy(c, mine, 4, at(x=pvx, ylo=other)))
         if DIRECT[c]:
-            other = 1 - ylo
-            for i, ri, t in ((3, 3, at(x=nxx, ylo=other)), (4, 4, at(x=pvx, ylo=other)),
-                             (5, 5 + ylo, at(x=far)), (6, 5 + ylo, at(x=far, ylo=other))):
-                go(gcopy(c, mine, i, t, ri))
+            go(gcopy(c, mine, 5, at(x=far), 5 + ylo))
+            go(gcopy(c, mine, 6, at(x=far, ylo=other), 5 + ylo))
         go(kcopy(c, 0, mine))
 
     xp, xm, yp = at(x=(x + 1) % 4), at(x=(x + 3) % 4), at(ylo=1 - ylo)
@@ -209,9 +216,6 @@
 
     def s_g2(c):
         gcopy(c, yours, 2, yp).wait_recv()
-        if not DIRECT[c]:
-            go(gcopy(c, yours, 3, xp))
-            go(gcopy(c, yours, 4, xm))
         go(kcopy(c, 3, yours))
 
     def s_g3(c):
@@ -249,7 +253,7 @@
             for k in range(8):
                 blk = xn.at[held[k], 1 - core, r, :]
                 rcopy(blk, blk, (k_s, k_r), (c, k), sib).wait_recv()
-        if c == 0:
+        if first_time(10 + g):
             for cp in lw[g]:
                 cp.wait()
         base, tile = 2 * span[g][0], 2 * (span[g][1] - span[g][0]) // SPLIT

time: 124 us -> 123 us (level)
  no operation moved by 1% of the time
where the time goes in v4:
time: 123 us
  Pallas kernels  122 us (99%)
    pallas_call x1, Pallas kernels, on_device(): pl.pallas_call(functools.partial(body, C), out_shape=(jax.ShapeDtypeStruc...  120 us

profile of v4, /device:TPU:1, one launch (start us, length us, event | category | flops | bytes accessed | tf_op | source)
XLA Modules:
  0.0 123.3 jit_solution(8445168611672154532)
XLA Ops:
  0.6 120.3 %layer.1 = (f32[64,2048]{1,0:T(8,128)}, f32[2,64,1664]{2,1,0:T(8,128)}) custom-call(bf16[2,64,512]{2,1,0:T(8,128)(2,1)} %bitcast.4, bf16[64,2048]{1,0:T(8,128)(2,1)} %rin_h.1, bf16[512,2048]{1,0:T(8,128)(2,1)} %wo_h.1, f32[1,2048]{1,0:T(1,128)} %bitcast.5, bf16[2048,1664]{1,0:T(8,128)(2,1)} %wg_h.1, bf16[2048,1664]{1,0:T(8,128)(2,1)} %wu_h.1), custom_call_target="tpu_custom_call" | custom-call | tf_op jit(solution)/shard_map/layer/pallas_call | solution.py:350
  121.0 2.1 %handover.1 = (f32[64,2048]{1,0:T(8,128)}, f32[128,1664]{1,0:T(8,128)}) custom-call(f32[64,2048]{1,0:T(8,128)} %get-tuple-element.4.res_h, f32[128,1664]{1,0:T(8,128)} %bitcast.3), custom_call_target="tpu_custom_call" | custom-call | tf_op jit(solution)/shard_map/handover/pallas_call | solution.py:370

commit v5 on v4

--- a/solution.py
+++ b/solution.py
@@ -18,15 +18,15 @@
 
 
 ORDER = [
-    (0, 0), (0, 1), (0, 2), (0, 3), (1, 0), (1, 1), (0, 5), (2, 0), (2, 1), (3, 0), (1, 2), (3, 1), (0, 4), (2, 2),
-    (4, 1), (4, 0), (1, 3), (3, 2), (2, 3), (5, 1), (5, 0), (1, 4), (6, 1), (4, 2), (3, 3), (7, 1), (1, 5), (8, 1),
-    (6, 0), (5, 2), (4, 3), (9, 1), (2, 4), (6, 2), (10, 1), (7, 0), (8, 0), (11, 1), (9, 0), (3, 4), (5, 3),
-    (10, 0), (7, 2), (8, 2), (2, 5), (11, 0), (6, 3), (4, 4), (12, 1), (9, 2), (12, 0), (3, 5), (13, 0), (13, 1),
-    (10, 2), (7, 3), (8, 3), (5, 4), (11, 2), (4, 5), (12, 2), (14, 1), (9, 3), (5, 5), (13, 2), (6, 4), (10, 3),
-    (14, 0), (11, 3), (14, 2), (7, 4), (8, 4), (6, 5), (9, 4), (7, 5), (8, 5), (12, 3), (15, 2), (15, 0), (13, 3),
-    (16, 2), (9, 5), (10, 4), (15, 1), (10, 5), (14, 3), (11, 5), (12, 5), (11, 4), (16, 1), (12, 4), (17, 1),
-    (15, 3), (13, 5), (13, 4), (14, 5), (14, 4), (15, 5), (16, 3), (15, 4), (16, 0), (16, 5), (17, 3), (16, 4),
-    (17, 0), (17, 2), (17, 5), (17, 4),
+    (0, 0), (0, 1), (0, 5), (0, 2), (0, 3), (1, 0), (1, 1), (2, 0), (2, 1), (1, 5), (1, 2), (3, 0), (1, 3), (2, 2),
+    (0, 4), (4, 0), (3, 1), (3, 2), (5, 0), (2, 3), (4, 1), (6, 0), (4, 2), (5, 1), (7, 0), (3, 3), (6, 1), (2, 5),
+    (8, 0), (5, 2), (1, 4), (4, 3), (7, 1), (8, 1), (9, 0), (6, 2), (3, 5), (2, 4), (10, 0), (5, 3), (9, 1),
+    (11, 0), (10, 1), (7, 2), (8, 2), (4, 5), (11, 1), (6, 3), (12, 1), (9, 2), (3, 4), (12, 0), (5, 5), (13, 1),
+    (13, 0), (10, 2), (7, 3), (8, 3), (14, 1), (4, 4), (11, 2), (9, 3), (5, 4), (6, 5), (14, 0), (12, 2), (15, 0),
+    (10, 3), (6, 4), (11, 3), (7, 4), (7, 5), (12, 3), (8, 5), (8, 4), (13, 2), (13, 3), (15, 1), (9, 5), (9, 4),
+    (14, 2), (16, 1), (10, 4), (10, 5), (11, 5), (15, 2), (11, 4), (12, 4), (14, 3), (15, 3), (12, 5), (17, 1),
+    (13, 4), (13, 5), (16, 3), (16, 0), (14, 4), (17, 0), (14, 5), (16, 2), (15, 4), (17, 2), (15, 5), (16, 5),
+    (16, 4), (17, 3), (17, 4), (17, 5),
 ]
 
 

time: 123 us -> 125 us (1.016)
  Pallas kernels: 122 us -> 124 us
    pallas_call x1, Pallas kernels: 120 us -> 122 us  [on_device(): pl.pallas_call(functools.partial(body, C), out_shape=(jax.ShapeDtypeStruc...]
where the time goes in v5:
time: 125 us
  Pallas kernels  124 us (99%)
    pallas_call x1, Pallas kernels, on_device(): pl.pallas_call(functools.partial(body, C), out_shape=(jax.ShapeDtypeStruc...  122 us

profile of v5, /device:TPU:1, one launch (start us, length us, event | category | flops | bytes accessed | tf_op | source)
XLA Modules:
  0.0 125.3 jit_solution(17663210646177095311)
XLA Ops:
  0.6 122.3 %layer.1 = (f32[64,2048]{1,0:T(8,128)}, f32[2,64,1664]{2,1,0:T(8,128)}) custom-call(bf16[2,64,512]{2,1,0:T(8,128)(2,1)} %bitcast.4, bf16[64,2048]{1,0:T(8,128)(2,1)} %rin_h.1, bf16[512,2048]{1,0:T(8,128)(2,1)} %wo_h.1, f32[1,2048]{1,0:T(1,128)} %bitcast.5, bf16[2048,1664]{1,0:T(8,128)(2,1)} %wg_h.1, bf16[2048,1664]{1,0:T(8,128)(2,1)} %wu_h.1), custom_call_target="tpu_custom_call" | custom-call | tf_op jit(solution)/shard_map/layer/pallas_call | solution.py:350
  123.0 2.1 %handover.1 = (f32[64,2048]{1,0:T(8,128)}, f32[128,1664]{1,0:T(8,128)}) custom-call(f32[64,2048]{1,0:T(8,128)} %get-tuple-element.4.res_h, f32[128,1664]{1,0:T(8,128)} %bitcast.3), custom_call_target="tpu_custom_call" | custom-call | tf_op jit(solution)/shard_map/handover/pallas_call | solution.py:370
